TPU v7x, 256 devices: a whole 4x4x8 slice. The times are simulated.
256 devices in a mesh: scen: 8 (over x, y_hi), rows: 32 (over z, y_lo, core).
Axes of the slice: x: 4, y: 4 (y_hi: 2, y_lo: 2; y = y_hi * 2 + y_lo), z: 8, core: 2. Of those that a mesh axis runs over, the one named last changes fastest.
Arguments:
- factor_rows: float32 [32, 16384, 1024], P('scen', 'rows'), may hold values from -1.5 to 1.5
- panel_factor: float32 [32, 1024, 512], P('scen'), may hold values from -0.03125 to 0.03125
- pivot_add: float32 [512, 512], replicated, may hold values from -1 to 4, as said below
- trailing: float32 [16384, 4096], P('rows', 'scen'), may hold values from -6 to 6
Outputs:
- panel: float32 [16384, 512], P('rows')
- updated: float32 [16384, 4096], P('rows', 'scen')
Inputs may be any that keep to these rules, and one draw needn't show every extreme that they name: `pivot_add`: symmetric positive definite; its diagonal lies between 1 and 3 and its off-diagonal entries are small.
All inputs are finite; a program needn't handle non-finite values.
Results may differ from a plain program's by a relative error of at most 0.0001.
Values sent between devices are 32-bit elements; how exact they have to be, the bound alone decides.
No kernel may reach another device: no remote copies, remote signals or barrier semaphores. Data moves between devices by JAX's collectives and lax.ppermute only.
A program may use at most 128 MiB of HBM per device.

v0:
```python
import jax
import jax.numpy as jnp
from jax import lax
from jax.sharding import PartitionSpec as P

exact_mode = lax.Precision.HIGHEST


def gram_matrix(stacked):
    return lax.dot_general(
        stacked,
        stacked,
        (((0,), (0,)), ((), ())),
        precision=exact_mode,
        preferred_element_type=jnp.float32,
    )


def solve_rows(factor_chol, right_rows):
    return lax.linalg.triangular_solve(
        factor_chol, right_rows, left_side=False, lower=True, transpose_a=True
    )


def per_device(factor_rows, panel_factor, pivot_add, trailing):
    groups = panel_factor.shape[0]
    depth = panel_factor.shape[1]
    width = panel_factor.shape[2]
    block_rows = factor_rows.shape[1]
    row_share = block_rows // lax.axis_size("scen")
    local_gram = gram_matrix(panel_factor.reshape(groups * depth, width))
    pivot_block, whole = lax.psum(
        (
            local_gram,
            jnp.einsum(
                "grk,gkp->rp",
                factor_rows,
                panel_factor,
                precision=exact_mode,
                preferred_element_type=jnp.float32,
            ),
        ),
        "scen",
    )
    factor_chol = jnp.linalg.cholesky(pivot_block + pivot_add)
    block = solve_rows(factor_chol, whole)
    own_solved = lax.dynamic_slice_in_dim(block, lax.axis_index("scen") * row_share, row_share, 0)
    tile_width = trailing.shape[1] // lax.axis_size("rows")
    product = jnp.dot(
        block,
        lax.all_gather(own_solved[:tile_width], "rows", axis=0, tiled=True).T,
        precision=exact_mode,
        preferred_element_type=jnp.float32,
    )
    return (block, trailing - product)


def solution(mesh):
    return jax.shard_map(
        per_device,
        mesh=mesh,
        in_specs=(P("scen", "rows", None), P("scen", None, None), P(), P("rows", "scen")),
        out_specs=(P("rows", None), P("rows", "scen")),
        check_vma=False,
    )
```

profile of v0, /device:TPU:1, one launch (start us, length us, event | category | flops | bytes accessed | tf_op | source)
XLA Modules:
  0.0 381.4 jit_solution(4032874341552375634)
XLA Ops:
  7.2 17.5 %convolution_bitcast_fusion = f32[512,512]{0,1:T(8,128)} fusion(f32[4,1024,512]{2,1,0:T(8,128)} %param.5), kind=kOutput, calls=%fused_computation.3 | convolution fusion | flops 12884901888 | bytes 9437184 | tf_op jit(solution)/shard_map/dot_general | solution.py:10
  24.8 14.7 %convolution_bitcast_fusion.1 = f32[512,512]{1,0:T(8,128)} fusion(f32[4,512,1024]{2,1,0:T(8,128)S(1)} %copy-done.1, f32[4,1024,512]{2,1,0:T(8,128)S(1)} %copy-done), kind=kOutput, calls=%fused_computation.4 | convolution fusion | flops 12884901888 | bytes 17825792 | tf_op jit(solution)/shard_map/grk,gkp->rp/dot_general | solution.py:35
  40.4 116.0 %all-reduce.4.cloned.1.call-done = (f32[512,512]{1,0:T(8,128)}, f32[512,512]{0,1:T(8,128)}) async-done(((f32[512,512]{1,0:T(8,128)}, f32[512,512]{0,1:T(8,128)}), (f32[512,512]{1,0:T(8,128)}, f32[512,512]{0,1:T(8,128)})) %all-reduce.4.cloned.1.call-update) | async-done | bytes 2097168 | tf_op jit(solution)/shard_map/psum | solution.py:32
  156.3 1.4 add.50
  158.3 11.7 %cholesky.104 = f32[128,128]{1,0:T(8,128)S(1)} custom-call(f32[128,128]{1,0:T(8,128)S(1)} %cholesky.266), custom_call_target="Cholesky" | custom-call | tf_op jit(solution)/shard_map/jit(cholesky)/cholesky | solution.py:45
  170.1 9.8 %custom-call.30 = f32[1,128,128]{1,2,0:T(8,128)S(1)} custom-call(f32[1,128,128]{2,1,0:T(8,128)S(1)} %get-tuple-element.35), custom_call_target="InvertDiagBlocksLowerTriangular" | custom-call | tf_op jit(solution)/shard_map/jit(cholesky)/cholesky | solution.py:45
  180.7 11.7 %cholesky.217 = f32[128,128]{1,0:T(8,128)S(1)} custom-call(f32[128,128]{1,0:T(8,128)S(1)} %cholesky.270), custom_call_target="Cholesky" | custom-call | tf_op jit(solution)/shard_map/jit(cholesky)/cholesky | solution.py:45
  192.5 9.9 %custom-call.31 = f32[1,128,128]{1,2,0:T(8,128)S(1)} custom-call(f32[1,128,128]{2,1,0:T(8,128)S(1)} %get-tuple-element.32), custom_call_target="InvertDiagBlocksLowerTriangular" | custom-call | tf_op jit(solution)/shard_map/jit(cholesky)/cholesky | solution.py:45
  203.1 11.7 %cholesky.238 = f32[128,128]{1,0:T(8,128)S(1)} custom-call(f32[128,128]{1,0:T(8,128)S(1)} %cholesky.275), custom_call_target="Cholesky" | custom-call | tf_op jit(solution)/shard_map/jit(cholesky)/cholesky | solution.py:45
  214.8 0.7 compare_reduce_fusion.1
  215.6 9.8 %custom-call.32 = f32[1,128,128]{1,2,0:T(8,128)S(1)} custom-call(f32[1,128,128]{2,1,0:T(8,128)S(1)} %get-tuple-element.29), custom_call_target="InvertDiagBlocksLowerTriangular" | custom-call | tf_op jit(solution)/shard_map/jit(cholesky)/cholesky | solution.py:45
  226.0 11.9 %cholesky.255 = f32[128,128]{1,0:T(8,128)S(1)} custom-call(f32[128,128]{1,0:T(8,128)S(1)} %convolution_subtract_fusion.6), custom_call_target="Cholesky" | custom-call | tf_op jit(solution)/shard_map/jit(cholesky)/cholesky | solution.py:45
  237.9 0.6 compare_reduce_fusion
  238.5 0.6 compare_reduce_fusion.2
  241.9 10.4 %while.1 = (s32[]{:T(128)}, f32[512,512]{1,0:T(8,128)S(1)}, s32[4,2]{0,1:T(2,128)S(1)}, f32[4,128,128]{2,1,0:T(8,128)}, s32[]{:T(128)}) while((s32[]{:T(128)}, f32[512,512]{1,0:T(8,128)S(1)}, s32[4,2]{0,1:T(2,128)S(1)}, f32[4,128,128]{2,1,0:T(8,128)}, s32[]{:T(128)}) %tuple.33), condition=%wide.while_cond, body=%wide.while_body.sunk | while | flops 2 | bytes 132705 | solution.py:20
  242.0 0.5 fusion.42
  242.5 2.0 bitcast_dynamic-update-slice_fusion.2
  244.6 0.5 fusion.42
  245.1 2.0 bitcast_dynamic-update-slice_fusion.2
  247.2 0.5 fusion.42
  247.7 2.0 bitcast_dynamic-update-slice_fusion.2
  249.8 0.5 fusion.42
  250.3 2.0 bitcast_dynamic-update-slice_fusion.2
  252.3 40.1 %custom-call.33 = f32[4,128,128]{1,2,0:T(8,128)S(1)} custom-call(f32[4,128,128]{2,1,0:T(8,128)} %get-tuple-element.9), custom_call_target="InvertDiagBlocksLowerTriangular" | custom-call | tf_op jit(solution)/shard_map/triangular_solve | solution.py:20
  292.4 1.4 fusion.10
  293.8 1.5 convolution_subtract_fusion.2
  295.8 1.9 convolution_subtract_fusion.1
  298.1 2.4 convolution_subtract_fusion.3
  301.2 0.7 copy.15
  301.9 1.3 copy.16
  303.2 65.4 %all-gather.2.cloned.1.call-done = f32[512,512]{1,0:T(8,128)} async-done(((f32[16,512]{1,0:T(8,128)}), f32[512,512]{1,0:T(8,128)}) %all-gather.2.cloned.1.call-update) | async-done | bytes 1048592 | tf_op jit(solution)/shard_map/all_gather | solution.py:51
  368.6 5.7 %convolution_subtract_fusion = f32[512,512]{1,0:T(8,128)} fusion(f32[512,512]{1,0:T(8,128)S(1)} %copy-done.3, f32[512,512]{1,0:T(8,128)} %all-gather.2.cloned.1.call-done, f32[512,128]{0,1:T(8,128)S(1)} %fusion.19, f32[512,128]{0,1:T(8,128)S(1)} %fusion.20, f32[512,128]{0,1:T(8,128)S(1)} %fusion.21, f32[512,128]{0,1:T(8,128)S(1)} %fusion.10), kind=kOutput, calls=%fused_computation.2 | convolution fusion | flops 1611661312 | bytes 4194304 | tf_op jit(solution)/shard_map/dot_general | solution.py:49
  (42 shorter events, 5.5 us)
Async XLA Ops:
  7.2 149.2 %all-reduce.4.cloned.1.call-start = ((), (), s32[]{:S(2)}) async-start(), calls=%async_computation.1 | async-start | bytes 4194304 | tf_op jit(solution)/shard_map/psum | solution.py:32
  7.2 17.5 %copy-start = (f32[4,1024,512]{2,1,0:T(8,128)S(1)}, f32[4,1024,512]{2,1,0:T(8,128)}, u32[]{:S(2)}) copy-start(f32[4,1024,512]{2,1,0:T(8,128)} %param.5) | copy-start | bytes 25165828
  7.2 17.5 %copy-start.1 = (f32[4,512,1024]{2,1,0:T(8,128)S(1)}, f32[4,512,1024]{2,1,0:T(8,128)}, u32[]{:S(2)}) copy-start(f32[4,512,1024]{2,1,0:T(8,128)} %param.4) | copy-start | bytes 25165828
  24.8 15.2 %copy-start.2 = (f32[512,512]{1,0:T(8,128)S(1)}, f32[512,512]{1,0:T(8,128)}, u32[]{:S(2)}) copy-start(f32[512,512]{1,0:T(8,128)} %param.6) | copy-start | bytes 3145732
  39.5 329.1 %all-gather.2.cloned.1.call-start = ((), (), s32[]{:S(2)}) async-start(), calls=%async_computation | async-start | bytes 1081344 | tf_op jit(solution)/shard_map/all_gather | solution.py:51
  180.3 188.3 %copy-start.3 = (f32[512,512]{1,0:T(8,128)S(1)}, f32[512,512]{1,0:T(8,128)}, u32[]{:S(2)}) copy-start(f32[512,512]{1,0:T(8,128)} %param.7) | copy-start | bytes 3145732
Sparse Core Ops, SparseCore 0:
  39.6 116.6 all-reduce.3
  302.1 66.5 all-gather.1
where the time goes:
time: 387 us; the launch traced here: 381 us
  waiting for transfers between devices  181 us (47%)
  other arithmetic  121 us (31%)
  matrix products  48.2 us (12%)
  between operations  17.1 us (4%)
  local copies, waits for them, and re-layouts  13.4 us (3%)
    psum x1, waiting for transfers between devices, per_device(): lax.psum((local_gram, jnp.einsum('grk,gkp->rp', factor_rows, panel_factor...  116 us
    another operation x14, other arithmetic, per_device(): factor_chol = jnp.linalg.cholesky(pivot_block + pivot_add)  78.7 us
    all_gather x1, waiting for transfers between devices, per_device(): lax.all_gather(own_solved[:tile_width], 'rows', axis=0, tiled=True)  65.4 us
    another operation x4, other arithmetic, solve_rows(): lax.linalg.triangular_solve(factor_chol, right_rows, left_side=False, low...  40.3 us
    dot_general x1, matrix products, gram_matrix(): lax.dot_general(stacked, stacked, (((0,), (0,)), ((), ())), precision=exa...  17.5 us
    dot_general x1, matrix products, per_device(): jnp.einsum('grk,gkp->rp', factor_rows, panel_factor, precision=exact_mode...  14.7 us
    another operation x12, local copies, waits for them, and re-layouts  10.4 us
    another operation x7, matrix products, solve_rows(): lax.linalg.triangular_solve(factor_chol, right_rows, left_side=False, low...  8.5 us
  transfers between devices with their start and end apart: 2, of which 2 were waited for; matrix products, arithmetic and copies ran while one was open for 0% of the time, Pallas kernels for 0%

commit v1 on v0

--- a/solution.py
+++ b/solution.py
@@ -48,7 +48,12 @@
     tile_width = trailing.shape[1] // lax.axis_size("rows")
     product = jnp.dot(
         block,
-        lax.all_gather(own_solved[:tile_width], "rows", axis=0, tiled=True).T,
+        jnp.concatenate(
+            lax.all_to_all(
+                jnp.stack([own_solved[:tile_width]] * lax.axis_size("rows")), "rows", 0, 0
+            ),
+            axis=0,
+        ).T,
         precision=exact_mode,
         preferred_element_type=jnp.float32,
     )

time: 387 us -> 358 us (0.925)
  waiting for transfers between devices: 181 us -> 143 us
  starting transfers between devices: 0.55 us -> 11.3 us
    all_gather x1 -> x0, waiting for transfers between devices: 65.4 us -> none  [per_device(): lax.all_gather(own_solved[:tile_width], 'rows', axis=0, tiled=True)]
    all_to_all x0 -> x1, waiting for transfers between devices: none -> 26.8 us  [per_device(): lax.all_to_all(jnp.stack([own_solved[:tile_width]] * lax.axis_size('rows'...]
    all_to_all x0 -> x1, starting transfers between devices: none -> 11.2 us  [per_device(): lax.all_to_all(jnp.stack([own_solved[:tile_width]] * lax.axis_size('rows'...]
    another operation x12 -> x13, local copies, waits for them, and re-layouts: 10.4 us -> 9.03 us
where the time goes in v1:
time: 358 us; the launch traced here: 352 us
  waiting for transfers between devices  143 us (40%)
  other arithmetic  120 us (34%)
  matrix products  48.7 us (14%)
  between operations  17.1 us (5%)
  local copies, waits for them, and re-layouts  11.4 us (3%)
  starting transfers between devices  11.3 us (3%)
    psum x1, waiting for transfers between devices, per_device(): lax.psum((local_gram, jnp.einsum('grk,gkp->rp', factor_rows, panel_factor...  116 us
    another operation x14, other arithmetic, per_device(): factor_chol = jnp.linalg.cholesky(pivot_block + pivot_add)  78.8 us
    another operation x4, other arithmetic, solve_rows(): lax.linalg.triangular_solve(factor_chol, right_rows, left_side=False, low...  39.5 us
    all_to_all x1, waiting for transfers between devices, per_device(): lax.all_to_all(jnp.stack([own_solved[:tile_width]] * lax.axis_size('rows'...  26.8 us
    dot_general x1, matrix products, gram_matrix(): lax.dot_general(stacked, stacked, (((0,), (0,)), ((), ())), precision=exa...  17.5 us
    dot_general x1, matrix products, per_device(): jnp.einsum('grk,gkp->rp', factor_rows, panel_factor, precision=exact_mode...  15.1 us
    all_to_all x1, starting transfers between devices, per_device(): lax.all_to_all(jnp.stack([own_solved[:tile_width]] * lax.axis_size('rows'...  11.2 us
    another operation x7, matrix products, solve_rows(): lax.linalg.triangular_solve(factor_chol, right_rows, left_side=False, low...  8.49 us
  transfers between devices with their start and end apart: 2, of which 2 were waited for; matrix products, arithmetic and copies ran while one was open for 0% of the time, Pallas kernels for 0%

profile of v1, /device:TPU:1, one launch (start us, length us, event | category | flops | bytes accessed | tf_op | source)
XLA Modules:
  0.0 351.7 jit_solution(1069825765688010520)
XLA Ops:
  7.2 17.5 %convolution_bitcast_fusion = f32[512,512]{0,1:T(8,128)} fusion(f32[4,1024,512]{2,1,0:T(8,128)} %param.5), kind=kOutput, calls=%fused_computation.3 | convolution fusion | flops 12884901888 | bytes 9437184 | tf_op jit(solution)/shard_map/dot_general | solution.py:10
  24.8 15.1 %convolution_bitcast_fusion.1 = f32[512,512]{1,0:T(8,128)} fusion(f32[4,512,1024]{2,1,0:T(8,128)S(1)} %copy-done.1, f32[4,1024,512]{2,1,0:T(8,128)S(1)} %copy-done), kind=kOutput, calls=%fused_computation.4 | convolution fusion | flops 12884901888 | bytes 17825792 | tf_op jit(solution)/shard_map/grk,gkp->rp/dot_general | solution.py:35
  40.3 116.5 %all-reduce.4.cloned.1.call-done = (f32[512,512]{1,0:T(8,128)}, f32[512,512]{0,1:T(8,128)}) async-done(((f32[512,512]{1,0:T(8,128)}, f32[512,512]{0,1:T(8,128)}), (f32[512,512]{1,0:T(8,128)}, f32[512,512]{0,1:T(8,128)})) %all-reduce.4.cloned.1.call-update) | async-done | bytes 2097168 | tf_op jit(solution)/shard_map/psum | solution.py:32
  156.8 1.4 add.50
  158.8 11.7 %cholesky.104 = f32[128,128]{1,0:T(8,128)S(1)} custom-call(f32[128,128]{1,0:T(8,128)S(1)} %cholesky.266), custom_call_target="Cholesky" | custom-call | tf_op jit(solution)/shard_map/jit(cholesky)/cholesky | solution.py:45
  170.5 9.8 %custom-call.30 = f32[1,128,128]{1,2,0:T(8,128)S(1)} custom-call(f32[1,128,128]{2,1,0:T(8,128)S(1)} %get-tuple-element.33), custom_call_target="InvertDiagBlocksLowerTriangular" | custom-call | tf_op jit(solution)/shard_map/jit(cholesky)/cholesky | solution.py:45
  181.1 11.7 %cholesky.217 = f32[128,128]{1,0:T(8,128)S(1)} custom-call(f32[128,128]{1,0:T(8,128)S(1)} %cholesky.270), custom_call_target="Cholesky" | custom-call | tf_op jit(solution)/shard_map/jit(cholesky)/cholesky | solution.py:45
  192.9 10.0 %custom-call.31 = f32[1,128,128]{1,2,0:T(8,128)S(1)} custom-call(f32[1,128,128]{2,1,0:T(8,128)S(1)} %get-tuple-element.30), custom_call_target="InvertDiagBlocksLowerTriangular" | custom-call | tf_op jit(solution)/shard_map/jit(cholesky)/cholesky | solution.py:45
  203.5 11.7 %cholesky.238 = f32[128,128]{1,0:T(8,128)S(1)} custom-call(f32[128,128]{1,0:T(8,128)S(1)} %cholesky.275), custom_call_target="Cholesky" | custom-call | tf_op jit(solution)/shard_map/jit(cholesky)/cholesky | solution.py:45
  215.3 0.7 compare_reduce_fusion.1
  216.0 9.8 %custom-call.32 = f32[1,128,128]{1,2,0:T(8,128)S(1)} custom-call(f32[1,128,128]{2,1,0:T(8,128)S(1)} %get-tuple-element.27), custom_call_target="InvertDiagBlocksLowerTriangular" | custom-call | tf_op jit(solution)/shard_map/jit(cholesky)/cholesky | solution.py:45
  226.4 11.9 %cholesky.255 = f32[128,128]{1,0:T(8,128)S(1)} custom-call(f32[128,128]{1,0:T(8,128)S(1)} %convolution_subtract_fusion.6), custom_call_target="Cholesky" | custom-call | tf_op jit(solution)/shard_map/jit(cholesky)/cholesky | solution.py:45
  238.4 0.6 compare_reduce_fusion
  239.0 0.6 compare_reduce_fusion.2
  242.3 8.0 %while.1 = (s32[]{:T(128)}, f32[512,512]{1,0:T(8,128)S(1)}, s32[4,2]{0,1:T(2,128)S(1)}, f32[4,128,128]{2,1,0:T(8,128)S(1)}, s32[]{:T(128)}) while((s32[]{:T(128)}, f32[512,512]{1,0:T(8,128)S(1)}, s32[4,2]{0,1:T(2,128)S(1)}, f32[4,128,128]{2,1,0:T(8,128)S(1)}, s32[]{:T(128)}) %tuple.32), condition=%wide.while_cond, body=%wide.while_body.sunk | while | flops 2 | bytes 131181 | solution.py:20
  242.4 0.5 fusion.42
  242.9 1.4 bitcast_dynamic-update-slice_fusion.2
  244.4 0.5 fusion.42
  244.9 1.4 bitcast_dynamic-update-slice_fusion.2
  246.4 0.5 fusion.42
  246.9 1.4 bitcast_dynamic-update-slice_fusion.2
  248.9 1.4 bitcast_dynamic-update-slice_fusion.2
  250.3 39.3 %custom-call.33 = f32[4,128,128]{1,2,0:T(8,128)S(1)} custom-call(f32[4,128,128]{2,1,0:T(8,128)S(1)} %get-tuple-element.9), custom_call_target="InvertDiagBlocksLowerTriangular" | custom-call | tf_op jit(solution)/shard_map/triangular_solve | solution.py:20
  289.7 1.4 fusion.10
  291.0 1.5 convolution_subtract_fusion.2
  293.0 1.9 convolution_subtract_fusion.1
  295.4 2.4 convolution_subtract_fusion.3
  298.5 1.1 stack.2
  299.6 11.2 %all-to-all-start = ((f32[32,16,512]{2,1,0:T(8,128)}), f32[32,16,512]{2,1,0:T(8,128)S(1)}, u32[]{:S(2)}, u32[]{:S(2)}) async-start(f32[32,16,512]{2,1,0:T(8,128)} %stack.2), calls=%async_computation | async-start | bytes 2097152 | tf_op jit(solution)/shard_map/all_to_all | solution.py:52
  310.9 1.3 copy.11
  312.2 26.8 %all-to-all-done = f32[32,16,512]{2,1,0:T(8,128)S(1)} async-done(((f32[32,16,512]{2,1,0:T(8,128)}), f32[32,16,512]{2,1,0:T(8,128)S(1)}, u32[]{:S(2)}, u32[]{:S(2)}) %all-to-all-start) | async-done | bytes 1048608 | tf_op jit(solution)/shard_map/all_to_all | solution.py:52
  339.0 5.7 %convolution_subtract_fusion = f32[512,512]{1,0:T(8,128)} fusion(f32[512,512]{1,0:T(8,128)} %param.7, f32[512,512]{1,0:T(8,128)S(1)} %bitcast.58, f32[512,128]{0,1:T(8,128)S(1)} %fusion.19, f32[512,128]{0,1:T(8,128)S(1)} %fusion.20, f32[512,128]{0,1:T(8,128)S(1)} %fusion.21, f32[512,128]{0,1:T(8,128)S(1)} %fusion.10), kind=kOutput, calls=%fused_computation.2 | convolution fusion | flops 1611661312 | bytes 4194304 | tf_op jit(solution)/shard_map/dot_general | solution.py:49
  (40 shorter events, 5.6 us)
Async XLA Ops:
  7.2 149.6 %all-reduce.4.cloned.1.call-start = ((), (), s32[]{:S(2)}) async-start(), calls=%async_computation.1 | async-start | bytes 4194304 | tf_op jit(solution)/shard_map/psum | solution.py:32
  7.2 17.5 %copy-start = (f32[4,1024,512]{2,1,0:T(8,128)S(1)}, f32[4,1024,512]{2,1,0:T(8,128)}, u32[]{:S(2)}) copy-start(f32[4,1024,512]{2,1,0:T(8,128)} %param.5) | copy-start | bytes 25165828
  7.2 17.5 %copy-start.1 = (f32[4,512,1024]{2,1,0:T(8,128)S(1)}, f32[4,512,1024]{2,1,0:T(8,128)}, u32[]{:S(2)}) copy-start(f32[4,512,1024]{2,1,0:T(8,128)} %param.4) | copy-start | bytes 25165828
  24.8 15.2 %copy-start.2 = (f32[512,512]{1,0:T(8,128)S(1)}, f32[512,512]{1,0:T(8,128)}, u32[]{:S(2)}) copy-start(f32[512,512]{1,0:T(8,128)} %param.6) | copy-start | bytes 3145732
  299.6 39.3 %all-to-all-start = ((f32[32,16,512]{2,1,0:T(8,128)}), f32[32,16,512]{2,1,0:T(8,128)S(1)}, u32[]{:S(2)}, u32[]{:S(2)}) async-start(f32[32,16,512]{2,1,0:T(8,128)} %stack.2), calls=%async_computation | async-start | bytes 2097152 | tf_op jit(solution)/shard_map/all_to_all | solution.py:52
Sparse Core Ops, SparseCore 0:
  40.0 116.6 all-reduce.3
